TPU v7x, 256 devices: a whole 4x4x8 slice. The times are simulated.
256 devices in a mesh: seq: 128 (over x, y_lo, z, core), chan: 2 (over y_hi).
Axes of the slice: x: 4, y: 4 (y_hi: 2, y_lo: 2; y = y_hi * 2 + y_lo), z: 8, core: 2. Of those that a mesh axis runs over, the one named last changes fastest.
Arguments:
- tokens: int32 [16384], P('seq'), may hold values from 0 to 3
- stem_weight: bfloat16 [5, 4, 768], replicated, may hold values from -2.5 to 2.5
- conv_weight: bfloat16 [5, 768, 768], P(None, None, 'chan'), may hold values from -0.09375 to 0.09375
- cotangent: bfloat16 [16384, 768], P('seq', 'chan'), may hold values from -6 to 6
Outputs:
- blended: bfloat16 [16384, 768], P('seq', 'chan')
- grad_conv: float32 [5, 768, 768], P(None, 'seq', 'chan')
- grad_stem: float32 [5, 4, 768], P(None, None, 'chan')
All inputs are finite; a program needn't handle non-finite values.
Results may differ from a plain program's by a relative error of at most 0.012.
Values may be sent and summed in bfloat16 or wider, within the bound.
A program may use at most 128 MiB of HBM per device.

v0:
```python
import math
import jax
import jax.numpy as jnp
from jax import lax
from jax.sharding import PartitionSpec as P


def from_partner(value, axis, distance):
    mask = 2**distance
    pairs = [(source, source ^ mask) for source in range(lax.axis_size(axis))]
    return lax.ppermute(value, axis, pairs)


def padded(block, sides, width):
    for axis, dim in sides:
        count = lax.axis_size(axis)
        forward = [(i, i + 1) for i in range(count - 1)]
        backward = [(target, source) for source, target in forward]
        low = lax.ppermute(
            lax.slice_in_dim(block, block.shape[dim] - width, None, axis=dim), axis, forward
        )
        high = lax.ppermute(lax.slice_in_dim(block, 0, width, axis=dim), axis, backward)
        block = jnp.concatenate([low, block, high], axis=dim)
    return block


def gelu_parts(values_in):
    coeff = math.sqrt(2.0 / math.pi)
    tanh_val = jnp.tanh(coeff * (values_in + 0.044715 * values_in**3))
    result = 0.5 * values_in * (1.0 + tanh_val)
    slopes = 0.5 * (1.0 + tanh_val) + 0.5 * values_in * (1.0 - tanh_val**2) * coeff * (
        1.0 + 3.0 * 0.044715 * values_in**2
    )
    return (result, slopes)


def on_device(tokens, stem_weight, conv_weight, cotangent):
    positions = tokens.shape[0]
    full_width = conv_weight.shape[1]
    half_width = conv_weight.shape[2]
    taps = conv_weight.shape[0]
    shards = lax.axis_size("seq")
    chan_start = lax.axis_index("chan") * half_width
    dir_grad = cotangent * 0.5
    moved_bases = tokens.astype(jnp.bfloat16)
    moved_cot = cotangent
    for bit_pos in range(shards.bit_length() - 1):
        moved_bases, moved_cot = from_partner((moved_bases, moved_cot), "seq", bit_pos)
    rc_ids = 4 - jnp.flip(moved_bases, 0).astype(jnp.int32)
    rc_grad = jnp.flip(moved_cot, 0) * 0.5
    stem_pair = jnp.stack([stem_weight, stem_weight])
    conv_pair = jnp.stack([conv_weight, conv_weight])
    letter_ids = jnp.stack([tokens + 1, rc_ids])
    wide_ids = padded(letter_ids, (("seq", 1),), 4)
    one_hot = (wide_ids[:, :, None] == jnp.arange(1, 5, dtype=jnp.int32)[None, None, :]).astype(
        jnp.bfloat16
    )
    span = positions + 4
    stem_sum = jnp.zeros((2, span, full_width), jnp.float32)
    for k in range(taps):
        stem_sum = stem_sum + jnp.einsum(
            "spv,svc->spc",
            one_hot[:, k : k + span],
            stem_pair[:, k],
            preferred_element_type=jnp.float32,
        )
    stem_act = stem_sum.astype(jnp.bfloat16)
    place = lax.axis_index("seq") * positions - 2 + jnp.arange(span, dtype=jnp.int32)
    inside = (place >= 0) & (place < positions * shards)
    gelu_val, gelu_slope = gelu_parts(stem_act.astype(jnp.float32))
    act = jnp.where(inside[None, :, None], gelu_val, 0.0).astype(jnp.bfloat16)
    conv_sum = jnp.zeros((2, positions, half_width), jnp.float32)
    for k in range(taps):
        conv_sum = conv_sum + jnp.einsum(
            "spc,scd->spd",
            act[:, k : k + positions],
            conv_pair[:, k],
            preferred_element_type=jnp.float32,
        )
    own_stem = lax.dynamic_slice_in_dim(
        stem_act[:, 2 : positions + 2], chan_start, half_width, 2
    ).astype(jnp.float32)
    layer_out = own_stem + conv_sum
    moved_out = layer_out[1]
    for bit_pos in range(shards.bit_length() - 1):
        moved_out = from_partner(moved_out, "seq", bit_pos)
    rc_out = jnp.flip(moved_out, 0)
    blended = (0.5 * (layer_out[0] + rc_out)).astype(jnp.bfloat16)
    out_grad = jnp.stack([dir_grad, rc_grad])
    wide_grad = padded(out_grad, (("seq", 1),), 2)
    kernel_list = []
    for k in range(taps):
        kernel_list.append(
            jnp.einsum(
                "spc,spd->scd",
                act[:, k : k + positions],
                out_grad,
                preferred_element_type=jnp.float32,
            )
        )
    kernel_grad = jnp.stack(kernel_list, axis=1)
    slope_rows = gelu_slope[:, 2 : positions + 2]
    own_hot = [one_hot[:, k + 2 : k + 2 + positions].astype(jnp.float32) for k in range(taps)]
    data_part = jnp.zeros((2, positions, full_width), jnp.float32)
    for k in range(taps):
        data_part = data_part + jnp.einsum(
            "spd,scd->spc",
            wide_grad[:, 4 - k : 4 - k + positions],
            conv_pair[:, k],
            preferred_element_type=jnp.float32,
        )
    data_full = lax.psum(data_part, "chan")
    stem_in = data_full * slope_rows
    stem_list = []
    for k in range(taps):
        stem_list.append(
            jnp.einsum("spv,spc->svc", own_hot[k], stem_in, precision=lax.Precision.HIGHEST)
        )
    stem_grad = lax.dynamic_slice_in_dim(jnp.stack(stem_list, axis=1), chan_start, half_width, 3)
    grad_conv = jnp.sum(
        lax.psum_scatter(kernel_grad, "seq", scatter_dimension=2, tiled=True), axis=0
    )
    grad_stem = lax.psum(stem_grad[0] + stem_grad[1], "seq")
    return (blended, grad_conv, grad_stem)


def solution(mesh):
    return jax.shard_map(
        on_device,
        mesh=mesh,
        in_specs=(P("seq"), P(), P(None, None, "chan"), P("seq", "chan")),
        out_specs=(P("seq", "chan"), P(None, "seq", "chan"), P(None, None, "chan")),
        check_vma=False,
    )
```

profile of v0, /device:TPU:1, one launch (start us, length us, event | category | flops | bytes accessed | tf_op | source)
XLA Modules:
  0.0 1273.7 jit_solution(16065917112089102861)
XLA Ops:
  7.9 3.2 collective-permute-start
  12.0 4.0 fusion.11
  16.0 3.0 collective-permute-start.2
  19.9 5.4 collective-permute-start.3
  31.0 2.7 collective-permute-start.6
  35.1 9.0 collective-permute-start.7
  46.0 2.9 collective-permute-done.8
  52.8 4.5 collective-permute-start.18
  57.7 3.2 collective-permute-done.18
  62.5 6.6 collective-permute-done.19
  69.1 4.6 collective-permute-start.20
  79.2 2.7 collective-permute-start.22
  82.0 2.4 fusion.20
  85.3 5.5 collective-permute-start.23
  90.8 2.1 collective-permute-start.24
  92.9 1.9 bitcast_dynamic-update-slice_fusion.4
  101.4 2.9 bitcast_dynamic-update-slice_fusion.2
  104.3 2.0 bitcast_dynamic-update-slice_fusion.1
  106.3 2.0 bitcast_dynamic-update-slice_fusion
  108.3 20.7 %copy.23 = f32[2,5,768,384]{3,0,1,2:T(2,128)} copy(f32[2,5,768,384]{3,2,0,1:T(8,128)} %bitcast_dynamic-update-slice_fusion) | data formatting | bytes 23592960 | tf_op jit(solution)/shard_map/stack | solution.py:101
  136.7 6.2 collective-permute-done.10
  142.9 2.4 collective-permute-start.11
  145.3 9.5 collective-permute-done.11
  154.9 3.1 collective-permute-start.12
  158.0 12.2 collective-permute-done.12
  170.6 6.3 collective-permute-done.13
  177.6 4.3 collective-permute-done.14
  181.9 2.8 collective-permute-start.15
  185.9 2.3 collective-permute-done.15
  189.9 2.4 fusion.22
  194.2 545.5 %psum.15 = f32[5,4,384]{2,1,0:T(4,128)} all-reduce(f32[5,4,384]{2,1,0:T(4,128)S(1)} %fusion.47), channel_id=1, replica_groups=mesh['seq'=128,'chan'=2] {'seq'}, use_global_device_ids=true, to_apply=%region_3.4 | all-reduce | flops 7680 | bytes 61440 | tf_op jit(solution)/shard_map/psum | solution.py:123
  739.7 525.6 %all-reduce.6.cloned.1.call-done = f32[2,5,768,384]{3,0,1,2:T(2,128)} async-done(((f32[2,5,768,384]{3,0,1,2:T(2,128)}), f32[2,5,768,384]{3,0,1,2:T(2,128)}) %all-reduce.6.cloned.1.call-update) | async-done | bytes 11796496
  (101 shorter events, 44.5 us)
Async XLA Ops:
  7.2 182.7 %all-reduce.4.cloned.1.call-start = ((), (), s32[]{:S(2)}) async-start(), calls=%async_computation | async-start | bytes 1572864 | tf_op jit(solution)/shard_map/psum | solution.py:112
  7.9 4.1 collective-permute-start
  11.2 37.9 %collective-permute-start.16 = (bf16[128,384]{1,0:T(8,128)(2,1)}, bf16[128,384]{1,0:T(8,128)(2,1)S(1)}, u32[]{:S(2)}, u32[]{:S(2)}) collective-permute-start(bf16[128,384]{1,0:T(8,128)(2,1)} %param.7), channel_id=1, source_target_pairs={{0,2},{2,0},{4,6},{6,4},{8,10},{10,8},{12,14},{14,12},{16,18},{18,... | collective-permute-start | bytes 294920 | tf_op jit(solution)/shard_map/ppermute | solution.py:11
  12.0 4.0 collective-permute-start.1
  12.0 6.9 copy-start.11
  12.0 45.3 %copy-start.10 = (bf16[5,4,768]{2,1,0:T(4,128)(2,1)S(1)}, bf16[5,4,768]{2,1,0:T(4,128)(2,1)}, u32[]{:S(2)}) copy-start(bf16[5,4,768]{2,1,0:T(4,128)(2,1)} %param.5) | copy-start | bytes 92164
  16.0 3.9 collective-permute-start.2
  19.9 6.3 collective-permute-start.3
  26.2 2.4 collective-permute-start.4
  28.6 2.4 collective-permute-start.5
  31.0 3.9 collective-permute-start.6
  35.1 11.0 collective-permute-start.7
  44.1 4.9 collective-permute-start.8
  49.1 3.8 collective-permute-start.17
  52.8 8.1 collective-permute-start.18
  60.9 8.2 collective-permute-start.19
  69.1 6.6 collective-permute-start.20
  75.8 3.5 collective-permute-start.21
  79.2 5.9 collective-permute-start.22
  85.2 12.0 copy-start.6
  85.3 12.0 collective-permute-start.23
  90.8 6.5 collective-permute-start.24
  101.4 1163.9 %all-reduce.6.cloned.1.call-start = ((), (), s32[]{:S(2)}) async-start(), calls=%async_computation.1 | async-start | bytes 23592960
  133.9 50.8 %copy-start.12 = (u32[256]{0:T(256)S(1)}, u32[256]{0:T(256)}, u32[]{:S(2)}) copy-start(u32[256]{0:T(256)} %constant.44) | copy-start | bytes 3076
  135.0 54.9 %copy-start.8 = (f32[2,132,768]{2,1,0:T(8,128)S(1)}, f32[2,132,768]{2,1,0:T(8,128)}, u32[]{:S(2)}) copy-start(f32[2,132,768]{2,1,0:T(8,128)} %get-tuple-element.9) | copy-start | bytes 2433028
  135.1 1.6 collective-permute-start.9
  136.7 6.2 collective-permute-start.10
  142.9 12.0 collective-permute-start.11
  154.9 15.4 %collective-permute-start.12 = (f32[128,384]{1,0:T(8,128)S(1)}, f32[128,384]{1,0:T(8,128)S(1)}, u32[]{:S(2)}, u32[]{:S(2)}) collective-permute-start(f32[128,384]{1,0:T(8,128)S(1)} %collective-permute-done.11), channel_id=1, source_target_pairs={{0,16},{2,18},{4,20},{6,22},{8,24},{10,26},{12,28},{14,30},{16,0},... | collective-permute-start | bytes 589832 | tf_op jit(solution)/shard_map/ppermute | solution.py:11
  170.3 6.7 collective-permute-start.13
  176.9 5.0 collective-permute-start.14
  181.9 6.3 collective-permute-start.15
  (8 other events, 15.9 us)
Sparse Core Ops, SparseCore 0:
  101.5 47.3 all-reduce.3
  151.8 1113.4 all-reduce.5
where the time goes:
time: 1270 us
  waiting for transfers between devices  593 us (47%)
  blocking collectives  545 us (43%)
  starting transfers between devices  61.4 us (5%)
  local copies, waits for them, and re-layouts  26.1 us (2%)
  matrix products  23.2 us (2%)
  between operations  15 us (1%)
    psum x1, blocking collectives, on_device(): grad_stem = lax.psum(stem_grad[0] + stem_grad[1], 'seq')  545 us
    unnamed x3, waiting for transfers between devices  526 us
    ppermute x21, waiting for transfers between devices, from_partner(): return lax.ppermute(value, axis, pairs)  64 us
    ppermute x21, starting transfers between devices, from_partner(): return lax.ppermute(value, axis, pairs)  42.8 us
  transfers between devices with their start and end apart: 27, of which 21 were waited for; matrix products, arithmetic and copies ran while one was open for 4% of the time, Pallas kernels for 0%

commit v1 on v0

--- a/solution.py
+++ b/solution.py
@@ -120,7 +120,7 @@
     grad_conv = jnp.sum(
         lax.psum_scatter(kernel_grad, "seq", scatter_dimension=2, tiled=True), axis=0
     )
-    grad_stem = lax.psum(stem_grad[0] + stem_grad[1], "seq")
+    grad_stem = jnp.sum(lax.all_gather(stem_grad[0] + stem_grad[1], "seq"), axis=0)
     return (blended, grad_conv, grad_stem)
 
 

time: 1270 us -> 1490 us (1.17)
  waiting for transfers between devices: 593 us -> 1350 us
  blocking collectives: 545 us -> 0 us
    unnamed x3 -> x4, waiting for transfers between devices: 526 us -> 1110 us
    psum x1 -> x0, blocking collectives: 545 us -> none  [on_device(): grad_stem = lax.psum(stem_grad[0] + stem_grad[1], 'seq')]
    all_gather x0 -> x1, waiting for transfers between devices: none -> 141 us  [on_device(): lax.all_gather(stem_grad[0] + stem_grad[1], 'seq')]
    psum x1, waiting for transfers between devices: 0.01 us -> 44.6 us  [on_device(): data_full = lax.psum(data_part, 'chan')]
  transfers between devices with their start and end apart: 27 -> 28, of which waited for: 21 -> 21; matrix products, arithmetic and copies ran while one was open for 4% -> 3% of each run, Pallas kernels for 0% -> 0%
where the time goes in v1:
time: 1490 us
  waiting for transfers between devices  1350 us (91%)
  starting transfers between devices  66.8 us (4%)
  local copies, waits for them, and re-layouts  20.9 us (1%)
  matrix products  19.4 us (1%)
    unnamed x4, waiting for transfers between devices  1110 us
    all_gather x1, waiting for transfers between devices, on_device(): lax.all_gather(stem_grad[0] + stem_grad[1], 'seq')  141 us
    ppermute x21, waiting for transfers between devices, from_partner(): return lax.ppermute(value, axis, pairs)  55.9 us
    psum x1, waiting for transfers between devices, on_device(): data_full = lax.psum(data_part, 'chan')  44.6 us
    ppermute x21, starting transfers between devices, from_partner(): return lax.ppermute(value, axis, pairs)  40.3 us
  transfers between devices with their start and end apart: 28, of which 21 were waited for; matrix products, arithmetic and copies ran while one was open for 3% of the time, Pallas kernels for 0%

profile of v1, /device:TPU:1, one launch (start us, length us, event | category | flops | bytes accessed | tf_op | source)
XLA Modules:
  0.0 1491.0 jit_solution(15212997318172782641)
XLA Ops:
  7.9 3.2 collective-permute-start
  11.2 4.1 fusion.11
  15.4 2.4 collective-permute-done.1
  19.2 1.9 collective-permute-done.2
  21.1 5.2 collective-permute-start.3
  32.1 2.5 collective-permute-start.6
  36.8 2.9 collective-permute-done.17
  41.2 12.1 collective-permute-start.7
  53.3 1.9 collective-permute-start.8
  55.2 4.3 collective-permute-start.19
  59.6 3.2 collective-permute-done.19
  64.2 2.1 collective-permute-done.20
  69.8 3.0 collective-permute-start.22
  75.0 10.3 collective-permute-start.23
  85.3 1.9 collective-permute-start.24
  87.2 1.8 fusion.80
  95.2 2.4 fusion.20
  97.6 44.6 %all-reduce.4.cloned.1.call-done = f32[2,128,768]{2,1,0:T(8,128)} async-done(((f32[2,128,768]{2,1,0:T(8,128)}), f32[2,128,768]{2,1,0:T(8,128)}) %all-reduce.4.cloned.1.call-update) | async-done | bytes 786448 | tf_op jit(solution)/shard_map/psum | solution.py:112
  142.3 2.6 fusion.22
  151.0 15.7 %copy.23 = f32[2,5,768,384]{3,0,1,2:T(2,128)} copy(f32[2,5,768,384]{3,2,0,1:T(8,128)S(1)} %bitcast_dynamic-update-slice_fusion) | data formatting | bytes 23592960 | tf_op jit(solution)/shard_map/stack | solution.py:101
  175.9 5.6 collective-permute-done.10
  181.5 2.0 collective-permute-start.11
  183.4 9.7 collective-permute-done.11
  193.1 6.2 collective-permute-start.12
  199.4 7.9 collective-permute-done.12
  207.3 4.5 collective-permute-done.13
  211.8 1.9 collective-permute-start.14
  213.7 3.6 collective-permute-done.14
  219.9 3.6 collective-permute-done.15
  225.2 141.2 %all-gather.2.cloned.1.call-done = f32[128,5,4,384]{3,2,0,1:T(4,128)} async-done(((f32[1,5,4,384]{3,2,0,1:T(4,128)}), f32[128,5,4,384]{3,2,0,1:T(4,128)}) %all-gather.2.cloned.1.call-update) | async-done | bytes 3932176 | tf_op jit(solution)/shard_map/all_gather | solution.py:123
  366.4 3.2 reduce_sum.19
  369.7 1113.2 %all-reduce.6.cloned.1.call-done = f32[2,5,768,384]{3,0,1,2:T(2,128)} async-done(((f32[2,5,768,384]{3,0,1,2:T(2,128)}), f32[2,5,768,384]{3,0,1,2:T(2,128)}) %all-reduce.6.cloned.1.call-update) | async-done | bytes 11796496
  (100 shorter events, 45.5 us)
Async XLA Ops:
  7.2 135.1 %all-reduce.4.cloned.1.call-start = ((), (), s32[]{:S(2)}) async-start(), calls=%async_computation | async-start | bytes 1572864 | tf_op jit(solution)/shard_map/psum | solution.py:112
  7.9 7.3 collective-permute-start
  11.2 25.0 %collective-permute-start.16 = (bf16[128,384]{1,0:T(8,128)(2,1)}, bf16[128,384]{1,0:T(8,128)(2,1)S(1)}, u32[]{:S(2)}, u32[]{:S(2)}) collective-permute-start(bf16[128,384]{1,0:T(8,128)(2,1)} %param.7), channel_id=1, source_target_pairs={{0,2},{2,0},{4,6},{6,4},{8,10},{10,8},{12,14},{14,12},{16,18},{18,... | collective-permute-start | bytes 294920 | tf_op jit(solution)/shard_map/ppermute | solution.py:11
  11.2 56.6 %copy-start.8 = (bf16[5,4,768]{2,1,0:T(4,128)(2,1)S(1)}, bf16[5,4,768]{2,1,0:T(4,128)(2,1)}, u32[]{:S(2)}) copy-start(bf16[5,4,768]{2,1,0:T(4,128)(2,1)} %param.5) | copy-start | bytes 92164
  15.3 2.5 collective-permute-start.1
  17.8 3.3 collective-permute-start.2
  21.1 6.3 collective-permute-start.3
  27.4 2.4 collective-permute-start.4
  29.8 2.4 collective-permute-start.5
  32.1 3.9 collective-permute-start.6
  36.2 3.5 collective-permute-start.17
  39.7 15.5 %collective-permute-start.18 = (bf16[128,384]{1,0:T(8,128)(2,1)S(1)}, bf16[128,384]{1,0:T(8,128)(2,1)S(1)}, u32[]{:S(2)}, u32[]{:S(2)}) collective-permute-start(bf16[128,384]{1,0:T(8,128)(2,1)S(1)} %collective-permute-done.17), channel_id=1, source_target_pairs={{0,8},{2,10},{4,12},{6,14},{8,0},{10,2},{12,4},{14,6},{16,24},{18,... | collective-permute-start | bytes 294920 | tf_op jit(solution)/shard_map/ppermute | solution.py:11
  41.2 18.3 %collective-permute-start.7 = (s32[2,4]{1,0:T(2,128)S(1)}, s32[2,4]{1,0:T(2,128)S(1)}, u32[]{:S(2)}, u32[]{:S(2)}) collective-permute-start(s32[2,4]{1,0:T(2,128)S(1)} %get-tuple-element.18), channel_id=1, source_target_pairs={{0,2},{2,4},{4,6},{6,8},{8,10},{10,12},{12,14},{14,16},{16,18},{18... | collective-permute-start | bytes 104 | tf_op jit(solution)/shard_map/ppermute | solution.py:19
  53.3 6.2 collective-permute-start.8
  55.2 7.6 collective-permute-start.19
  62.8 3.5 collective-permute-start.20
  66.3 3.5 collective-permute-start.21
  69.8 5.0 collective-permute-start.22
  74.9 14.1 copy-start.5
  74.9 14.2 copy-start
  75.0 14.1 collective-permute-start.23
  85.3 3.7 collective-permute-start.24
  93.0 273.4 %all-gather.2.cloned.1.call-start = ((), (), s32[]{:S(2)}) async-start(), calls=%async_computation.1 | async-start | bytes 3962880 | tf_op jit(solution)/shard_map/all_gather | solution.py:123
  147.4 1335.4 %all-reduce.6.cloned.1.call-start = ((), (), s32[]{:S(2)}) async-start(), calls=%async_computation.2 | async-start | bytes 23592960
  171.6 47.0 %copy-start.10 = (u32[256]{0:T(256)S(1)}, u32[256]{0:T(256)}, u32[]{:S(2)}) copy-start(u32[256]{0:T(256)} %constant.44) | copy-start | bytes 3076
  172.8 1.8 collective-permute-start.9
  174.6 6.9 collective-permute-start.10
  181.5 11.7 collective-permute-start.11
  193.1 14.2 collective-permute-start.12
  207.3 4.5 collective-permute-start.13
  211.8 5.4 collective-permute-start.14
  217.3 6.2 collective-permute-start.15
  (7 other events, 12.0 us)
Sparse Core Ops, SparseCore 0:
  93.1 49.0 all-reduce.3
  147.5 218.8 all-gather.1
  369.3 1113.5 all-reduce.5
